TPU v7x, 128 devices: a whole 4x4x4 slice. The times are simulated.
128 devices in a mesh: stream: 16 (over z, y), passage: 4 (over x_hi, core), span: 2 (over x_lo).
Axes of the slice: x: 4 (x_hi: 2, x_lo: 2; x = x_hi * 2 + x_lo), y: 4, z: 4, core: 2. Of those that a mesh axis runs over, the one named last changes fastest.
Arguments:
- residual: float32 [6, 32, 256, 256], P(None, 'stream', 'passage', 'span'), may hold values from -4 to 4
- dq_old: float32 [6, 32, 256, 256], P(None, 'stream', 'passage', 'span'), may hold values from -6 to 6
- lateral_coef: float32 [32, 256, 256], P('stream', 'passage', 'span'), may hold values from 0.05 to 0.25
- diag_inverse: float32 [6, 6, 32, 256, 256], P(None, None, 'stream', 'passage', 'span'), may hold values from -1 to 1.2, as said below
- match_list: int32 [16, 256], P('stream', 'passage'), may hold values from 0 to 255, as said below
- slide_weight: float32 [256], P('passage'), may hold values from 0 to 1
Outputs:
- dq_new: float32 [6, 32, 256, 256], P(None, 'stream', 'passage', 'span')
Inputs may be any that keep to these rules, and one draw needn't show every extreme that they name: match_list[b, p] = (p + offset_b) mod 256, where offset_b = (offset_0 + b * 64) mod 256. `diag_inverse`: each 6x6 block is a diagonal scaling of the identity plus a small antisymmetric part.
All inputs are finite; a program needn't handle non-finite values.
Results may differ from a plain program's by a relative error of at most 0.00013.
Values sent between devices are 32-bit elements; how exact they have to be, the bound alone decides.
No kernel may reach another device: no remote copies, remote signals or barrier semaphores. Data moves between devices by JAX's collectives and lax.ppermute only.
A program may use at most 320 MiB of HBM per device.

v0:
```python
import jax
import jax.numpy as jnp
from jax import lax
from jax.sharding import PartitionSpec as P


def padded(x, sides, width, wrap):
    for axis, dim in sides:
        peers, length = (lax.axis_size(axis), x.shape[dim])
        up = [(i, (i + 1) % peers) for i in range(peers if wrap else peers - 1)]
        down = [(j, i) for i, j in up]
        last = lax.slice_in_dim(x, length - width, length, axis=dim)
        first = lax.slice_in_dim(x, 0, width, axis=dim)
        before = lax.ppermute(last, axis, up)
        after = lax.ppermute(first, axis, down)
        x = jnp.concatenate([before, x, after], axis=dim)
    return x


def passed_along(block, axis, distance):
    devices = range(lax.axis_size(axis))
    route = [((i - distance) % len(devices), i) for i in devices]
    return lax.ppermute(block, axis, route)


def shifted(block, axis, distance):
    devices = range(lax.axis_size(axis))
    route = [(i - distance, i) for i in devices if i - distance in devices]
    return lax.ppermute(block, axis, route)


def apply_block(matrix, vector):
    return jnp.einsum("ab...,b...->a...", matrix, vector, precision=lax.Precision.HIGHEST)


def compose(later, earlier):
    return jnp.einsum("ab...,bc...->ac...", later, earlier, precision=lax.Precision.HIGHEST)


def plane_of(array, index, target_axis):
    return lax.dynamic_index_in_dim(array, index, target_axis, False)


def on_device(residual, dq_old, lateral_coef, diag_inverse, match_list, slide_weight):
    planes = residual.shape[1]
    beside_all = padded(dq_old, (("passage", 2),), 1, True)
    beside = padded(dq_old, (("span", 3),), 1, False)
    neighbours = (
        beside_all[:, :, 2:] + beside_all[:, :, :-2] + beside[:, :, :, 2:] + beside[:, :, :, :-2]
    )
    source = residual - lateral_coef[None] * neighbours
    face = dq_old[:, planes - 1]
    annulus = lax.all_gather(face, "passage", axis=1, tiled=True)
    upstream = passed_along(annulus, "stream", 1)
    total = upstream.shape[1]
    donors = match_list[0]
    nextidx = (donors + 1) % total
    weight = slide_weight[None, :, None]
    term = (1.0 - weight) * jnp.take(upstream, donors, axis=1) + weight * jnp.take(
        upstream, nextidx, axis=1
    )
    source = source.at[:, 0].add(term)
    first_inverse = diag_inverse[:, :, 0]
    start_maps = (first_inverse, apply_block(first_inverse, source[:, 0]))

    def lower_compose(index, carry):
        inverse = plane_of(diag_inverse, index, 2)
        given = plane_of(source, index, 1)
        return (compose(inverse, carry[0]), apply_block(inverse, carry[1] + given))

    lower_maps = lax.fori_loop(1, planes, lower_compose, start_maps)
    blocks = lax.axis_size("stream")

    def lower_pass(index, incoming):
        leaving = apply_block(lower_maps[0], incoming) + lower_maps[1]
        return shifted(leaving, "stream", 1)

    lower_in = lax.fori_loop(0, blocks - 1, lower_pass, jnp.zeros_like(lower_maps[1]))

    def lower_sweep(index, carry):
        current, lowers = carry
        inverse = plane_of(diag_inverse, index, 2)
        current = apply_block(inverse, plane_of(source, index, 1) + current)
        return (current, lax.dynamic_update_index_in_dim(lowers, current, index, 1))

    _, lowers = lax.fori_loop(0, planes, lower_sweep, (lower_in, jnp.zeros_like(source)))
    last_inverse = diag_inverse[:, :, planes - 1]
    top_maps = (last_inverse, lowers[:, planes - 1])

    def upper_compose(step, carry):
        index = planes - 1 - step
        inverse = plane_of(diag_inverse, index, 2)
        return (
            compose(inverse, carry[0]),
            plane_of(lowers, index, 1) + apply_block(inverse, carry[1]),
        )

    upper_maps = lax.fori_loop(1, planes, upper_compose, top_maps)

    def upper_pass(index, incoming):
        leaving = apply_block(upper_maps[0], incoming) + upper_maps[1]
        return shifted(leaving, "stream", -1)

    upper_in = lax.fori_loop(0, blocks - 1, upper_pass, jnp.zeros_like(upper_maps[1]))

    def upper_sweep(step, carry):
        current, uppers = carry
        index = planes - 1 - step
        inverse = plane_of(diag_inverse, index, 2)
        current = plane_of(lowers, index, 1) + apply_block(inverse, current)
        return (current, lax.dynamic_update_index_in_dim(uppers, current, index, 1))

    _, uppers = lax.fori_loop(0, planes, upper_sweep, (upper_in, jnp.zeros_like(source)))
    return uppers


def solution(mesh):
    placed = (
        P(None, "stream", "passage", "span"),
        P(None, "stream", "passage", "span"),
        P("stream", "passage", "span"),
        P(None, None, "stream", "passage", "span"),
        P("stream", "passage"),
        P("passage"),
    )
    return jax.shard_map(
        on_device,
        mesh=mesh,
        in_specs=placed,
        out_specs=P(None, "stream", "passage", "span"),
        check_vma=False,
    )
```

profile of v0, /device:TPU:24, one launch (start us, length us, event | category | flops | bytes accessed | tf_op | source)
XLA Modules:
  0.0 680.0 jit_solution(18425378000636333673)
XLA Ops:
  3.8 5.4 collective-permute-start.5
  12.3 15.9 %all-gather = f32[6,1,256,128]{3,1,0,2:T(1,128)S(1)} all-gather(f32[6,1,64,128]{3,1,0,2:T(1,128)S(1)} %copy.144), channel_id=2, replica_groups=mesh['stream'=16,'passage'=4,'span'=2] {'passage'}, dimensions={2}, use_global_device_ids=true | all-gather | bytes 983040 | tf_op jit(solution)/shard_map/all_gather | solution.py:53
  32.2 14.8 %copy.143 = f32[6,6,1,64,128]{1,0,4,3,2:T(8,128)} copy(f32[6,6,1,64,128]{4,3,2,1,0:T(8,128)} %get-tuple-element.438) | data formatting | bytes 2359296
  47.0 14.9 %copy.142 = f32[6,6,1,64,128]{0,1,4,3,2:T(8,128)} copy(f32[6,6,1,64,128]{4,3,2,1,0:T(8,128)} %get-tuple-element.437) | data formatting | bytes 2359296
  62.0 71.8 %fusion.17 = f32[6,6,64,128]{0,1,3,2:T(8,128)} fusion(f32[6,6,1,64,128]{0,1,4,3,2:T(8,128)} %copy.142, f32[6,6,1,64,128]{1,0,4,3,2:T(8,128)} %copy.143), kind=kOutput, calls=%fused_computation.28 | convolution fusion | flops 21233664 | bytes 3538944 | tf_op jit(solution)/shard_map/while/body/eval_jaxpr/ab...,bc...->ac.../dot_general | solution.py:37
  133.8 61.7 %fusion.12 = f32[6,6,64,128]{0,1,3,2:T(8,128)} fusion(f32[6,6,1,64,128]{1,0,4,3,2:T(8,128)} %copy.143, f32[6,6,1,64,128]{0,1,4,3,2:T(8,128)} %copy.142), kind=kOutput, calls=%fused_computation.27 | convolution fusion | flops 21233664 | bytes 3538944 | tf_op jit(solution)/shard_map/while/body/eval_jaxpr/ab...,bc...->ac.../dot_general | solution.py:37
  195.7 15.6 %copy.82 = f32[6,6,64,128]{3,2,1,0:T(8,128)} copy(f32[6,6,64,128]{0,1,3,2:T(8,128)} %fusion.17) | data formatting | bytes 2359296 | tf_op jit(solution)/shard_map/while | solution.py:78
  211.3 15.4 %copy.85 = f32[6,6,64,128]{3,2,1,0:T(8,128)} copy(f32[6,6,64,128]{0,1,3,2:T(8,128)} %fusion.12) | data formatting | bytes 2359296 | tf_op jit(solution)/shard_map/while | solution.py:104
  237.6 2.7 copy.145
  240.3 15.3 %fusion.4 = f32[64,128,6]{2,1,0:T(8,128)} fusion(f32[6,6,1,64,128]{1,0,4,3,2:T(8,128)} %copy.143, f32[64,128,6]{2,1,0:T(8,128)} %copy.145), kind=kLoop, calls=%fused_computation.19 | loop fusion | flops 540672 | bytes 1572864
  255.6 2.8 copy.123
  260.6 2.7 copy.146
  263.2 16.8 %fusion.3 = f32[64,128,6]{2,1,0:T(8,128)} fusion(f32[6,6,1,64,128]{0,1,4,3,2:T(8,128)} %copy.142, f32[64,128,6]{2,1,0:T(8,128)} %copy.146), kind=kLoop, calls=%fused_computation.16 | loop fusion | flops 540672 | bytes 1572864
  280.0 2.9 copy.130
  282.9 170.6 %while.65 = (s32[]{:T(128)}, f32[6,64,128]{2,1,0:T(8,128)S(1)}, f32[6,6,64,128]{3,2,1,0:T(8,128)}, f32[6,64,128]{2,1,0:T(8,128)S(1)}, s32[]{:T(128)}) while((s32[]{:T(128)}, f32[6,64,128]{2,1,0:T(8,128)S(1)}, f32[6,6,64,128]{3,2,1,0:T(8,128)}, f32[6,64,128]{2,1,0:T(8,128)S(1)}, s32[]{:T(128)}) %tuple.133), condition=%wide.region_1.3_spmd, body=%wide.region_0.2_spmd.sunk | while | flops 589826 | bytes 2949221 | solution.py:78
  284.4 3.5 collective-permute-start
  287.9 5.8 collective-permute-done
  295.1 5.6 collective-permute-start
  300.7 4.0 collective-permute-done
  306.1 6.5 collective-permute-start
  312.6 3.2 collective-permute-done
  317.2 6.5 collective-permute-start
  323.8 3.2 collective-permute-done
  328.4 6.5 collective-permute-start
  334.9 3.2 collective-permute-done
  339.5 6.5 collective-permute-start
  346.0 3.2 collective-permute-done
  350.6 6.5 collective-permute-start
  357.1 3.2 collective-permute-done
  361.7 6.5 collective-permute-start
  368.2 3.2 collective-permute-done
  372.8 6.5 collective-permute-start
  379.3 4.3 collective-permute-done
  385.1 6.5 collective-permute-start
  391.6 5.1 collective-permute-done
  398.1 6.5 collective-permute-start
  404.6 4.2 collective-permute-done
  410.3 6.5 collective-permute-start
  416.8 3.4 collective-permute-done
  421.6 6.5 collective-permute-start
  428.1 3.2 collective-permute-done
  432.7 6.5 collective-permute-start
  439.2 3.2 collective-permute-done
  443.8 6.5 collective-permute-start
  450.3 3.2 collective-permute-done
  457.5 15.4 %fusion.5 = f32[64,128,6]{2,1,0:T(8,128)} fusion(f32[6,6,1,64,128]{1,0,4,3,2:T(8,128)} %copy.143, f32[64,128,6]{2,1,0:T(8,128)} %copy.147), kind=kLoop, calls=%fused_computation.20 | loop fusion | flops 540672 | bytes 1572864
  473.0 3.6 copy.137
  479.0 194.8 %while.67 = (s32[]{:T(128)}, f32[6,64,128]{2,1,0:T(8,128)}, f32[6,6,64,128]{3,2,1,0:T(8,128)S(1)}, f32[6,64,128]{2,1,0:T(8,128)}, s32[]{:T(128)}) while((s32[]{:T(128)}, f32[6,64,128]{2,1,0:T(8,128)}, f32[6,6,64,128]{3,2,1,0:T(8,128)S(1)}, f32[6,64,128]{2,1,0:T(8,128)}, s32[]{:T(128)}) %tuple.132), condition=%wide.region_5.7_spmd, body=%wide.region_4.6_spmd.sunk | while | flops 589826 | bytes 2949221 | solution.py:104
  483.6 8.5 %collective-permute-done.1 = f32[6,64,128]{2,1,0:T(8,128)} collective-permute-done((f32[6,64,128]{2,1,0:T(8,128)}, f32[6,64,128]{2,1,0:T(8,128)}, u32[]{:S(2)}, u32[]{:S(2)}) %collective-permute-start.1) | collective-permute-done | bytes 196640 | tf_op jit(solution)/shard_map/while/body/eval_jaxpr/ppermute | solution.py:29
  496.7 8.1 %collective-permute-done.1 = f32[6,64,128]{2,1,0:T(8,128)} collective-permute-done((f32[6,64,128]{2,1,0:T(8,128)}, f32[6,64,128]{2,1,0:T(8,128)}, u32[]{:S(2)}, u32[]{:S(2)}) %collective-permute-start.1) | collective-permute-done | bytes 196640 | tf_op jit(solution)/shard_map/while/body/eval_jaxpr/ppermute | solution.py:29
  509.4 8.1 %collective-permute-done.1 = f32[6,64,128]{2,1,0:T(8,128)} collective-permute-done((f32[6,64,128]{2,1,0:T(8,128)}, f32[6,64,128]{2,1,0:T(8,128)}, u32[]{:S(2)}, u32[]{:S(2)}) %collective-permute-start.1) | collective-permute-done | bytes 196640 | tf_op jit(solution)/shard_map/while/body/eval_jaxpr/ppermute | solution.py:29
  522.1 8.1 %collective-permute-done.1 = f32[6,64,128]{2,1,0:T(8,128)} collective-permute-done((f32[6,64,128]{2,1,0:T(8,128)}, f32[6,64,128]{2,1,0:T(8,128)}, u32[]{:S(2)}, u32[]{:S(2)}) %collective-permute-start.1) | collective-permute-done | bytes 196640 | tf_op jit(solution)/shard_map/while/body/eval_jaxpr/ppermute | solution.py:29
  534.8 8.1 %collective-permute-done.1 = f32[6,64,128]{2,1,0:T(8,128)} collective-permute-done((f32[6,64,128]{2,1,0:T(8,128)}, f32[6,64,128]{2,1,0:T(8,128)}, u32[]{:S(2)}, u32[]{:S(2)}) %collective-permute-start.1) | collective-permute-done | bytes 196640 | tf_op jit(solution)/shard_map/while/body/eval_jaxpr/ppermute | solution.py:29
  547.4 8.8 %collective-permute-done.1 = f32[6,64,128]{2,1,0:T(8,128)} collective-permute-done((f32[6,64,128]{2,1,0:T(8,128)}, f32[6,64,128]{2,1,0:T(8,128)}, u32[]{:S(2)}, u32[]{:S(2)}) %collective-permute-start.1) | collective-permute-done | bytes 196640 | tf_op jit(solution)/shard_map/while/body/eval_jaxpr/ppermute | solution.py:29
  560.8 9.9 %collective-permute-done.1 = f32[6,64,128]{2,1,0:T(8,128)} collective-permute-done((f32[6,64,128]{2,1,0:T(8,128)}, f32[6,64,128]{2,1,0:T(8,128)}, u32[]{:S(2)}, u32[]{:S(2)}) %collective-permute-start.1) | collective-permute-done | bytes 196640 | tf_op jit(solution)/shard_map/while/body/eval_jaxpr/ppermute | solution.py:29
  575.3 9.3 %collective-permute-done.1 = f32[6,64,128]{2,1,0:T(8,128)} collective-permute-done((f32[6,64,128]{2,1,0:T(8,128)}, f32[6,64,128]{2,1,0:T(8,128)}, u32[]{:S(2)}, u32[]{:S(2)}) %collective-permute-start.1) | collective-permute-done | bytes 196640 | tf_op jit(solution)/shard_map/while/body/eval_jaxpr/ppermute | solution.py:29
  589.3 8.5 %collective-permute-done.1 = f32[6,64,128]{2,1,0:T(8,128)} collective-permute-done((f32[6,64,128]{2,1,0:T(8,128)}, f32[6,64,128]{2,1,0:T(8,128)}, u32[]{:S(2)}, u32[]{:S(2)}) %collective-permute-start.1) | collective-permute-done | bytes 196640 | tf_op jit(solution)/shard_map/while/body/eval_jaxpr/ppermute | solution.py:29
  602.3 8.1 %collective-permute-done.1 = f32[6,64,128]{2,1,0:T(8,128)} collective-permute-done((f32[6,64,128]{2,1,0:T(8,128)}, f32[6,64,128]{2,1,0:T(8,128)}, u32[]{:S(2)}, u32[]{:S(2)}) %collective-permute-start.1) | collective-permute-done | bytes 196640 | tf_op jit(solution)/shard_map/while/body/eval_jaxpr/ppermute | solution.py:29
  615.0 8.1 %collective-permute-done.1 = f32[6,64,128]{2,1,0:T(8,128)} collective-permute-done((f32[6,64,128]{2,1,0:T(8,128)}, f32[6,64,128]{2,1,0:T(8,128)}, u32[]{:S(2)}, u32[]{:S(2)}) %collective-permute-start.1) | collective-permute-done | bytes 196640 | tf_op jit(solution)/shard_map/while/body/eval_jaxpr/ppermute | solution.py:29
  627.7 8.1 %collective-permute-done.1 = f32[6,64,128]{2,1,0:T(8,128)} collective-permute-done((f32[6,64,128]{2,1,0:T(8,128)}, f32[6,64,128]{2,1,0:T(8,128)}, u32[]{:S(2)}, u32[]{:S(2)}) %collective-permute-start.1) | collective-permute-done | bytes 196640 | tf_op jit(solution)/shard_map/while/body/eval_jaxpr/ppermute | solution.py:29
  640.3 8.1 %collective-permute-done.1 = f32[6,64,128]{2,1,0:T(8,128)} collective-permute-done((f32[6,64,128]{2,1,0:T(8,128)}, f32[6,64,128]{2,1,0:T(8,128)}, u32[]{:S(2)}, u32[]{:S(2)}) %collective-permute-start.1) | collective-permute-done | bytes 196640 | tf_op jit(solution)/shard_map/while/body/eval_jaxpr/ppermute | solution.py:29
  653.0 8.1 %collective-permute-done.1 = f32[6,64,128]{2,1,0:T(8,128)} collective-permute-done((f32[6,64,128]{2,1,0:T(8,128)}, f32[6,64,128]{2,1,0:T(8,128)}, u32[]{:S(2)}, u32[]{:S(2)}) %collective-permute-start.1) | collective-permute-done | bytes 196640 | tf_op jit(solution)/shard_map/while/body/eval_jaxpr/ppermute | solution.py:29
  665.7 8.1 %collective-permute-done.1 = f32[6,64,128]{2,1,0:T(8,128)} collective-permute-done((f32[6,64,128]{2,1,0:T(8,128)}, f32[6,64,128]{2,1,0:T(8,128)}, u32[]{:S(2)}, u32[]{:S(2)}) %collective-permute-start.1) | collective-permute-done | bytes 196640 | tf_op jit(solution)/shard_map/while/body/eval_jaxpr/ppermute | solution.py:29
  673.8 5.4 while.68
  (140 shorter events, 127.4 us)
Async XLA Ops:
  0.0 30.7 %copy-start = (f32[6,6,2,64,128]{4,3,2,1,0:T(8,128)S(1)}, f32[6,6,2,64,128]{4,3,2,1,0:T(8,128)}, u32[]{:S(2)}) copy-start(f32[6,6,2,64,128]{4,3,2,1,0:T(8,128)} %param.21) | copy-start | bytes 7077892
  2.5 224.2 %collective-permute-start.4 = (f32[6,2,64,1]{3,0,2,1:T(8,128)}, f32[6,2,64,1]{3,0,2,1:T(8,128)S(1)}, u32[]{:S(2)}, u32[]{:S(2)}) collective-permute-start(f32[6,2,64,1]{3,0,2,1:T(8,128)} %get-tuple-element.441), channel_id=1, source_target_pairs={{1,0},{3,2},{5,4},{7,6},{9,8},{11,10},{13,12},{15,14},{17,16},{19,... | collective-permute-start | bytes 9224 | tf_op jit(solution)/shard_map/ppermute | solution.py:15
  3.8 222.9 %collective-permute-start.5 = (f32[6,2,64,1]{3,0,2,1:T(8,128)}, f32[6,2,64,1]{3,0,2,1:T(8,128)}, u32[]{:S(2)}, u32[]{:S(2)}) collective-permute-start(f32[6,2,64,1]{3,0,2,1:T(8,128)} %get-tuple-element.442), channel_id=1, source_target_pairs={{0,1},{2,3},{4,5},{6,7},{8,9},{10,11},{12,13},{14,15},{16,17},{18,... | collective-permute-start | bytes 9224 | tf_op jit(solution)/shard_map/ppermute | solution.py:14
  9.2 217.5 %collective-permute-start.2 = (f32[6,2,1,128]{3,0,2,1:T(8,128)S(1)}, f32[6,2,1,128]{3,0,2,1:T(8,128)S(1)}, u32[]{:S(2)}, u32[]{:S(2)}) collective-permute-start(f32[6,2,1,128]{3,0,2,1:T(8,128)S(1)} %get-tuple-element.439), channel_id=1, source_target_pairs={{2,0},{4,2},{6,4},{0,6},{3,1},{5,3},{7,5},{1,7},{10,8},{12,10},{14... | collective-permute-start | bytes 18440 | tf_op jit(solution)/shard_map/ppermute | solution.py:15
  29.1 200.2 %collective-permute-start.6 = (f32[6,256,128]{2,1,0:T(8,128)}, f32[6,256,128]{2,1,0:T(8,128)}, u32[]{:S(2)}, u32[]{:S(2)}) collective-permute-start(f32[6,256,128]{2,1,0:T(8,128)} %bitcast.127), channel_id=1, source_target_pairs={{120,0},{0,8},{8,16},{16,24},{24,32},{32,40},{40,48},{48,56},{56,6... | collective-permute-start | bytes 2359304 | tf_op jit(solution)/shard_map/ppermute | solution.py:23
  133.8 61.7 %copy-start.8 = (s32[1,64]{1,0:T(1,128)S(1)}, s32[1,64]{1,0:T(1,128)}, u32[]{:S(2)}) copy-start(s32[1,64]{1,0:T(1,128)} %param.22) | copy-start | bytes 772
  133.8 61.8 %copy-start.7 = (f32[64]{0:T(128)S(1)}, f32[64]{0:T(128)}, u32[]{:S(2)}) copy-start(f32[64]{0:T(128)} %param.23) | copy-start | bytes 772
  195.5 32.0 %collective-permute-start.3 = (f32[6,2,1,128]{3,0,2,1:T(8,128)S(1)}, f32[6,2,1,128]{3,0,2,1:T(8,128)S(1)}, u32[]{:S(2)}, u32[]{:S(2)}) collective-permute-start(f32[6,2,1,128]{3,0,2,1:T(8,128)S(1)} %get-tuple-element.440), channel_id=1, source_target_pairs={{0,2},{2,4},{4,6},{6,0},{1,3},{3,5},{5,7},{7,1},{8,10},{10,12},{12... | collective-permute-start | bytes 18440 | tf_op jit(solution)/shard_map/ppermute | solution.py:14
  211.3 16.2 %copy-start.6 = (f32[2,64,128]{2,1,0:T(8,128)S(1)}, f32[2,64,128]{2,1,0:T(8,128)}, u32[]{:S(2)}) copy-start(f32[2,64,128]{2,1,0:T(8,128)} %param.20) | copy-start | bytes 196612
  226.7 0.8 copy-start.4
  237.6 18.0 %copy-start.2 = (f32[6,2,64,128]{3,0,2,1:T(8,128)}, f32[6,2,64,128]{3,0,2,1:T(8,128)S(1)}, u32[]{:S(2)}) copy-start(f32[6,2,64,128]{3,0,2,1:T(8,128)S(1)} %get-tuple-element.433) | copy-start | bytes 1179652
  284.4 9.3 %collective-permute-start = (f32[6,64,128]{2,1,0:T(8,128)S(1)}, f32[6,64,128]{2,1,0:T(8,128)S(1)}, u32[]{:S(2)}, u32[]{:S(2)}) collective-permute-start(f32[6,64,128]{2,1,0:T(8,128)S(1)} %bitcast_add_fusion.8), channel_id=1, source_target_pairs={{0,8},{8,16},{16,24},{24,32},{32,40},{40,48},{48,56},{56,64},{64,7... | collective-permute-start | bytes 589832 | tf_op jit(solution)/shard_map/while/body/eval_jaxpr/ppermute | solution.py:29
  295.1 9.6 %collective-permute-start = (f32[6,64,128]{2,1,0:T(8,128)S(1)}, f32[6,64,128]{2,1,0:T(8,128)S(1)}, u32[]{:S(2)}, u32[]{:S(2)}) collective-permute-start(f32[6,64,128]{2,1,0:T(8,128)S(1)} %bitcast_add_fusion.8), channel_id=1, source_target_pairs={{0,8},{8,16},{16,24},{24,32},{32,40},{40,48},{48,56},{56,64},{64,7... | collective-permute-start | bytes 589832 | tf_op jit(solution)/shard_map/while/body/eval_jaxpr/ppermute | solution.py:29
  306.1 9.7 %collective-permute-start = (f32[6,64,128]{2,1,0:T(8,128)S(1)}, f32[6,64,128]{2,1,0:T(8,128)S(1)}, u32[]{:S(2)}, u32[]{:S(2)}) collective-permute-start(f32[6,64,128]{2,1,0:T(8,128)S(1)} %bitcast_add_fusion.8), channel_id=1, source_target_pairs={{0,8},{8,16},{16,24},{24,32},{32,40},{40,48},{48,56},{56,64},{64,7... | collective-permute-start | bytes 589832 | tf_op jit(solution)/shard_map/while/body/eval_jaxpr/ppermute | solution.py:29
  317.2 9.7 %collective-permute-start = (f32[6,64,128]{2,1,0:T(8,128)S(1)}, f32[6,64,128]{2,1,0:T(8,128)S(1)}, u32[]{:S(2)}, u32[]{:S(2)}) collective-permute-start(f32[6,64,128]{2,1,0:T(8,128)S(1)} %bitcast_add_fusion.8), channel_id=1, source_target_pairs={{0,8},{8,16},{16,24},{24,32},{32,40},{40,48},{48,56},{56,64},{64,7... | collective-permute-start | bytes 589832 | tf_op jit(solution)/shard_map/while/body/eval_jaxpr/ppermute | solution.py:29
  328.4 9.7 %collective-permute-start = (f32[6,64,128]{2,1,0:T(8,128)S(1)}, f32[6,64,128]{2,1,0:T(8,128)S(1)}, u32[]{:S(2)}, u32[]{:S(2)}) collective-permute-start(f32[6,64,128]{2,1,0:T(8,128)S(1)} %bitcast_add_fusion.8), channel_id=1, source_target_pairs={{0,8},{8,16},{16,24},{24,32},{32,40},{40,48},{48,56},{56,64},{64,7... | collective-permute-start | bytes 589832 | tf_op jit(solution)/shard_map/while/body/eval_jaxpr/ppermute | solution.py:29
  339.5 9.7 %collective-permute-start = (f32[6,64,128]{2,1,0:T(8,128)S(1)}, f32[6,64,128]{2,1,0:T(8,128)S(1)}, u32[]{:S(2)}, u32[]{:S(2)}) collective-permute-start(f32[6,64,128]{2,1,0:T(8,128)S(1)} %bitcast_add_fusion.8), channel_id=1, source_target_pairs={{0,8},{8,16},{16,24},{24,32},{32,40},{40,48},{48,56},{56,64},{64,7... | collective-permute-start | bytes 589832 | tf_op jit(solution)/shard_map/while/body/eval_jaxpr/ppermute | solution.py:29
  350.6 9.7 %collective-permute-start = (f32[6,64,128]{2,1,0:T(8,128)S(1)}, f32[6,64,128]{2,1,0:T(8,128)S(1)}, u32[]{:S(2)}, u32[]{:S(2)}) collective-permute-start(f32[6,64,128]{2,1,0:T(8,128)S(1)} %bitcast_add_fusion.8), channel_id=1, source_target_pairs={{0,8},{8,16},{16,24},{24,32},{32,40},{40,48},{48,56},{56,64},{64,7... | collective-permute-start | bytes 589832 | tf_op jit(solution)/shard_map/while/body/eval_jaxpr/ppermute | solution.py:29
  361.7 9.7 %collective-permute-start = (f32[6,64,128]{2,1,0:T(8,128)S(1)}, f32[6,64,128]{2,1,0:T(8,128)S(1)}, u32[]{:S(2)}, u32[]{:S(2)}) collective-permute-start(f32[6,64,128]{2,1,0:T(8,128)S(1)} %bitcast_add_fusion.8), channel_id=1, source_target_pairs={{0,8},{8,16},{16,24},{24,32},{32,40},{40,48},{48,56},{56,64},{64,7... | collective-permute-start | bytes 589832 | tf_op jit(solution)/shard_map/while/body/eval_jaxpr/ppermute | solution.py:29
  372.8 10.8 %collective-permute-start = (f32[6,64,128]{2,1,0:T(8,128)S(1)}, f32[6,64,128]{2,1,0:T(8,128)S(1)}, u32[]{:S(2)}, u32[]{:S(2)}) collective-permute-start(f32[6,64,128]{2,1,0:T(8,128)S(1)} %bitcast_add_fusion.8), channel_id=1, source_target_pairs={{0,8},{8,16},{16,24},{24,32},{32,40},{40,48},{48,56},{56,64},{64,7... | collective-permute-start | bytes 589832 | tf_op jit(solution)/shard_map/while/body/eval_jaxpr/ppermute | solution.py:29
  385.1 11.6 %collective-permute-start = (f32[6,64,128]{2,1,0:T(8,128)S(1)}, f32[6,64,128]{2,1,0:T(8,128)S(1)}, u32[]{:S(2)}, u32[]{:S(2)}) collective-permute-start(f32[6,64,128]{2,1,0:T(8,128)S(1)} %bitcast_add_fusion.8), channel_id=1, source_target_pairs={{0,8},{8,16},{16,24},{24,32},{32,40},{40,48},{48,56},{56,64},{64,7... | collective-permute-start | bytes 589832 | tf_op jit(solution)/shard_map/while/body/eval_jaxpr/ppermute | solution.py:29
  398.1 10.7 %collective-permute-start = (f32[6,64,128]{2,1,0:T(8,128)S(1)}, f32[6,64,128]{2,1,0:T(8,128)S(1)}, u32[]{:S(2)}, u32[]{:S(2)}) collective-permute-start(f32[6,64,128]{2,1,0:T(8,128)S(1)} %bitcast_add_fusion.8), channel_id=1, source_target_pairs={{0,8},{8,16},{16,24},{24,32},{32,40},{40,48},{48,56},{56,64},{64,7... | collective-permute-start | bytes 589832 | tf_op jit(solution)/shard_map/while/body/eval_jaxpr/ppermute | solution.py:29
  410.3 9.9 %collective-permute-start = (f32[6,64,128]{2,1,0:T(8,128)S(1)}, f32[6,64,128]{2,1,0:T(8,128)S(1)}, u32[]{:S(2)}, u32[]{:S(2)}) collective-permute-start(f32[6,64,128]{2,1,0:T(8,128)S(1)} %bitcast_add_fusion.8), channel_id=1, source_target_pairs={{0,8},{8,16},{16,24},{24,32},{32,40},{40,48},{48,56},{56,64},{64,7... | collective-permute-start | bytes 589832 | tf_op jit(solution)/shard_map/while/body/eval_jaxpr/ppermute | solution.py:29
  421.6 9.7 %collective-permute-start = (f32[6,64,128]{2,1,0:T(8,128)S(1)}, f32[6,64,128]{2,1,0:T(8,128)S(1)}, u32[]{:S(2)}, u32[]{:S(2)}) collective-permute-start(f32[6,64,128]{2,1,0:T(8,128)S(1)} %bitcast_add_fusion.8), channel_id=1, source_target_pairs={{0,8},{8,16},{16,24},{24,32},{32,40},{40,48},{48,56},{56,64},{64,7... | collective-permute-start | bytes 589832 | tf_op jit(solution)/shard_map/while/body/eval_jaxpr/ppermute | solution.py:29
  432.7 9.7 %collective-permute-start = (f32[6,64,128]{2,1,0:T(8,128)S(1)}, f32[6,64,128]{2,1,0:T(8,128)S(1)}, u32[]{:S(2)}, u32[]{:S(2)}) collective-permute-start(f32[6,64,128]{2,1,0:T(8,128)S(1)} %bitcast_add_fusion.8), channel_id=1, source_target_pairs={{0,8},{8,16},{16,24},{24,32},{32,40},{40,48},{48,56},{56,64},{64,7... | collective-permute-start | bytes 589832 | tf_op jit(solution)/shard_map/while/body/eval_jaxpr/ppermute | solution.py:29
  443.8 9.7 %collective-permute-start = (f32[6,64,128]{2,1,0:T(8,128)S(1)}, f32[6,64,128]{2,1,0:T(8,128)S(1)}, u32[]{:S(2)}, u32[]{:S(2)}) collective-permute-start(f32[6,64,128]{2,1,0:T(8,128)S(1)} %bitcast_add_fusion.8), channel_id=1, source_target_pairs={{0,8},{8,16},{16,24},{24,32},{32,40},{40,48},{48,56},{56,64},{64,7... | collective-permute-start | bytes 589832 | tf_op jit(solution)/shard_map/while/body/eval_jaxpr/ppermute | solution.py:29
  454.0 3.6 copy-start.3
  473.0 6.0 copy-start.1
  481.7 10.4 %collective-permute-start.1 = (f32[6,64,128]{2,1,0:T(8,128)}, f32[6,64,128]{2,1,0:T(8,128)}, u32[]{:S(2)}, u32[]{:S(2)}) collective-permute-start(f32[6,64,128]{2,1,0:T(8,128)} %bitcast_add_fusion.9), channel_id=1, source_target_pairs={{8,0},{16,8},{24,16},{32,24},{40,32},{48,40},{56,48},{64,56},{72,6... | collective-permute-start | bytes 589832 | tf_op jit(solution)/shard_map/while/body/eval_jaxpr/ppermute | solution.py:29
  494.8 10.0 %collective-permute-start.1 = (f32[6,64,128]{2,1,0:T(8,128)}, f32[6,64,128]{2,1,0:T(8,128)}, u32[]{:S(2)}, u32[]{:S(2)}) collective-permute-start(f32[6,64,128]{2,1,0:T(8,128)} %bitcast_add_fusion.9), channel_id=1, source_target_pairs={{8,0},{16,8},{24,16},{32,24},{40,32},{48,40},{56,48},{64,56},{72,6... | collective-permute-start | bytes 589832 | tf_op jit(solution)/shard_map/while/body/eval_jaxpr/ppermute | solution.py:29
  507.5 10.0 %collective-permute-start.1 = (f32[6,64,128]{2,1,0:T(8,128)}, f32[6,64,128]{2,1,0:T(8,128)}, u32[]{:S(2)}, u32[]{:S(2)}) collective-permute-start(f32[6,64,128]{2,1,0:T(8,128)} %bitcast_add_fusion.9), channel_id=1, source_target_pairs={{8,0},{16,8},{24,16},{32,24},{40,32},{48,40},{56,48},{64,56},{72,6... | collective-permute-start | bytes 589832 | tf_op jit(solution)/shard_map/while/body/eval_jaxpr/ppermute | solution.py:29
  520.2 10.0 %collective-permute-start.1 = (f32[6,64,128]{2,1,0:T(8,128)}, f32[6,64,128]{2,1,0:T(8,128)}, u32[]{:S(2)}, u32[]{:S(2)}) collective-permute-start(f32[6,64,128]{2,1,0:T(8,128)} %bitcast_add_fusion.9), channel_id=1, source_target_pairs={{8,0},{16,8},{24,16},{32,24},{40,32},{48,40},{56,48},{64,56},{72,6... | collective-permute-start | bytes 589832 | tf_op jit(solution)/shard_map/while/body/eval_jaxpr/ppermute | solution.py:29
  532.8 10.0 %collective-permute-start.1 = (f32[6,64,128]{2,1,0:T(8,128)}, f32[6,64,128]{2,1,0:T(8,128)}, u32[]{:S(2)}, u32[]{:S(2)}) collective-permute-start(f32[6,64,128]{2,1,0:T(8,128)} %bitcast_add_fusion.9), channel_id=1, source_target_pairs={{8,0},{16,8},{24,16},{32,24},{40,32},{48,40},{56,48},{64,56},{72,6... | collective-permute-start | bytes 589832 | tf_op jit(solution)/shard_map/while/body/eval_jaxpr/ppermute | solution.py:29
  545.5 10.7 %collective-permute-start.1 = (f32[6,64,128]{2,1,0:T(8,128)}, f32[6,64,128]{2,1,0:T(8,128)}, u32[]{:S(2)}, u32[]{:S(2)}) collective-permute-start(f32[6,64,128]{2,1,0:T(8,128)} %bitcast_add_fusion.9), channel_id=1, source_target_pairs={{8,0},{16,8},{24,16},{32,24},{40,32},{48,40},{56,48},{64,56},{72,6... | collective-permute-start | bytes 589832 | tf_op jit(solution)/shard_map/while/body/eval_jaxpr/ppermute | solution.py:29
  558.9 11.8 %collective-permute-start.1 = (f32[6,64,128]{2,1,0:T(8,128)}, f32[6,64,128]{2,1,0:T(8,128)}, u32[]{:S(2)}, u32[]{:S(2)}) collective-permute-start(f32[6,64,128]{2,1,0:T(8,128)} %bitcast_add_fusion.9), channel_id=1, source_target_pairs={{8,0},{16,8},{24,16},{32,24},{40,32},{48,40},{56,48},{64,56},{72,6... | collective-permute-start | bytes 589832 | tf_op jit(solution)/shard_map/while/body/eval_jaxpr/ppermute | solution.py:29
  573.4 11.2 %collective-permute-start.1 = (f32[6,64,128]{2,1,0:T(8,128)}, f32[6,64,128]{2,1,0:T(8,128)}, u32[]{:S(2)}, u32[]{:S(2)}) collective-permute-start(f32[6,64,128]{2,1,0:T(8,128)} %bitcast_add_fusion.9), channel_id=1, source_target_pairs={{8,0},{16,8},{24,16},{32,24},{40,32},{48,40},{56,48},{64,56},{72,6... | collective-permute-start | bytes 589832 | tf_op jit(solution)/shard_map/while/body/eval_jaxpr/ppermute | solution.py:29
  587.3 10.4 %collective-permute-start.1 = (f32[6,64,128]{2,1,0:T(8,128)}, f32[6,64,128]{2,1,0:T(8,128)}, u32[]{:S(2)}, u32[]{:S(2)}) collective-permute-start(f32[6,64,128]{2,1,0:T(8,128)} %bitcast_add_fusion.9), channel_id=1, source_target_pairs={{8,0},{16,8},{24,16},{32,24},{40,32},{48,40},{56,48},{64,56},{72,6... | collective-permute-start | bytes 589832 | tf_op jit(solution)/shard_map/while/body/eval_jaxpr/ppermute | solution.py:29
  600.4 10.0 %collective-permute-start.1 = (f32[6,64,128]{2,1,0:T(8,128)}, f32[6,64,128]{2,1,0:T(8,128)}, u32[]{:S(2)}, u32[]{:S(2)}) collective-permute-start(f32[6,64,128]{2,1,0:T(8,128)} %bitcast_add_fusion.9), channel_id=1, source_target_pairs={{8,0},{16,8},{24,16},{32,24},{40,32},{48,40},{56,48},{64,56},{72,6... | collective-permute-start | bytes 589832 | tf_op jit(solution)/shard_map/while/body/eval_jaxpr/ppermute | solution.py:29
  613.1 10.0 %collective-permute-start.1 = (f32[6,64,128]{2,1,0:T(8,128)}, f32[6,64,128]{2,1,0:T(8,128)}, u32[]{:S(2)}, u32[]{:S(2)}) collective-permute-start(f32[6,64,128]{2,1,0:T(8,128)} %bitcast_add_fusion.9), channel_id=1, source_target_pairs={{8,0},{16,8},{24,16},{32,24},{40,32},{48,40},{56,48},{64,56},{72,6... | collective-permute-start | bytes 589832 | tf_op jit(solution)/shard_map/while/body/eval_jaxpr/ppermute | solution.py:29
  625.7 10.0 %collective-permute-start.1 = (f32[6,64,128]{2,1,0:T(8,128)}, f32[6,64,128]{2,1,0:T(8,128)}, u32[]{:S(2)}, u32[]{:S(2)}) collective-permute-start(f32[6,64,128]{2,1,0:T(8,128)} %bitcast_add_fusion.9), channel_id=1, source_target_pairs={{8,0},{16,8},{24,16},{32,24},{40,32},{48,40},{56,48},{64,56},{72,6... | collective-permute-start | bytes 589832 | tf_op jit(solution)/shard_map/while/body/eval_jaxpr/ppermute | solution.py:29
  638.4 10.0 %collective-permute-start.1 = (f32[6,64,128]{2,1,0:T(8,128)}, f32[6,64,128]{2,1,0:T(8,128)}, u32[]{:S(2)}, u32[]{:S(2)}) collective-permute-start(f32[6,64,128]{2,1,0:T(8,128)} %bitcast_add_fusion.9), channel_id=1, source_target_pairs={{8,0},{16,8},{24,16},{32,24},{40,32},{48,40},{56,48},{64,56},{72,6... | collective-permute-start | bytes 589832 | tf_op jit(solution)/shard_map/while/body/eval_jaxpr/ppermute | solution.py:29
  651.1 10.0 %collective-permute-start.1 = (f32[6,64,128]{2,1,0:T(8,128)}, f32[6,64,128]{2,1,0:T(8,128)}, u32[]{:S(2)}, u32[]{:S(2)}) collective-permute-start(f32[6,64,128]{2,1,0:T(8,128)} %bitcast_add_fusion.9), channel_id=1, source_target_pairs={{8,0},{16,8},{24,16},{32,24},{40,32},{48,40},{56,48},{64,56},{72,6... | collective-permute-start | bytes 589832 | tf_op jit(solution)/shard_map/while/body/eval_jaxpr/ppermute | solution.py:29
  663.8 10.0 %collective-permute-start.1 = (f32[6,64,128]{2,1,0:T(8,128)}, f32[6,64,128]{2,1,0:T(8,128)}, u32[]{:S(2)}, u32[]{:S(2)}) collective-permute-start(f32[6,64,128]{2,1,0:T(8,128)} %bitcast_add_fusion.9), channel_id=1, source_target_pairs={{8,0},{16,8},{24,16},{32,24},{40,32},{48,40},{56,48},{64,56},{72,6... | collective-permute-start | bytes 589832 | tf_op jit(solution)/shard_map/while/body/eval_jaxpr/ppermute | solution.py:29
  679.2 0.7 copy-start.5
where the time goes:
time: 683 us; the launch traced here: 680 us
  waiting for transfers between devices  181 us (27%)
  matrix products  134 us (20%)
  starting transfers between devices  133 us (19%)
  other arithmetic  121 us (18%)
  local copies, waits for them, and re-layouts  95.5 us (14%)
  blocking collectives  15.9 us (2%)
    ppermute x30, waiting for transfers between devices, shifted(): return lax.ppermute(block, axis, route)  181 us
    dot_general x2, matrix products, compose(): jnp.einsum('ab...,bc...->ac...', later, earlier, precision=lax.Precision....  134 us
    ppermute x30, starting transfers between devices, shifted(): return lax.ppermute(block, axis, route)  122 us
    unnamed x4, other arithmetic  48.5 us
    unnamed x26, local copies, waits for them, and re-layouts  40.9 us
    dot_general x34, other arithmetic, apply_block(): jnp.einsum('ab...,b...->a...', matrix, vector, precision=lax.Precision.HI...  39.4 us
    add x15, other arithmetic, upper_pass(): leaving = apply_block(upper_maps[0], incoming) + upper_maps[1]  24.4 us
    all_gather x1, blocking collectives, on_device(): annulus = lax.all_gather(face, 'passage', axis=1, tiled=True)  15.9 us
  transfers between devices with their start and end apart: 35, of which 30 were waited for; matrix products, arithmetic and copies ran while one was open for 29% of the time, Pallas kernels for 0%

commit v1 on v0

--- a/solution.py
+++ b/solution.py
@@ -2,6 +2,13 @@
 import jax.numpy as jnp
 from jax import lax
 from jax.sharding import PartitionSpec as P
+
+
+def gather_over(block, axis, along):
+    peers = lax.axis_size(axis)
+    pieces = jnp.stack([block for _ in range(peers)])
+    pieces = lax.all_to_all(pieces, axis, split_axis=0, concat_axis=0)
+    return jnp.concatenate(pieces, axis=along)
 
 
 def padded(x, sides, width, wrap):
@@ -50,7 +57,7 @@
     )
     source = residual - lateral_coef[None] * neighbours
     face = dq_old[:, planes - 1]
-    annulus = lax.all_gather(face, "passage", axis=1, tiled=True)
+    annulus = gather_over(face, "passage", 1)
     upstream = passed_along(annulus, "stream", 1)
     total = upstream.shape[1]
     donors = match_list[0]

time: 683 us -> 676 us (0.990)
  blocking collectives: 15.9 us -> 0 us
    all_gather x1 -> x0, blocking collectives: 15.9 us -> none  [on_device(): annulus = lax.all_gather(face, 'passage', axis=1, tiled=True)]
    unnamed x26 -> x25, local copies, waits for them, and re-layouts: 40.9 us -> 40.8 us
  transfers between devices with their start and end apart: 35 -> 36, of which waited for: 30 -> 30; matrix products, arithmetic and copies ran while one was open for 29% -> 30% of each run, Pallas kernels for 0% -> 0%
where the time goes in v1:
time: 676 us; the launch traced here: 673 us
  waiting for transfers between devices  183 us (27%)
  starting transfers between devices  137 us (20%)
  matrix products  134 us (20%)
  other arithmetic  121 us (18%)
  local copies, waits for them, and re-layouts  97.6 us (14%)
    ppermute x30, waiting for transfers between devices, shifted(): return lax.ppermute(block, axis, route)  183 us
    dot_general x2, matrix products, compose(): jnp.einsum('ab...,bc...->ac...', later, earlier, precision=lax.Precision....  134 us
    ppermute x30, starting transfers between devices, shifted(): return lax.ppermute(block, axis, route)  122 us
    unnamed x4, other arithmetic  48.5 us
    unnamed x25, local copies, waits for them, and re-layouts  40.8 us
    dot_general x34, other arithmetic, apply_block(): jnp.einsum('ab...,b...->a...', matrix, vector, precision=lax.Precision.HI...  39.4 us
    add x15, other arithmetic, upper_pass(): leaving = apply_block(upper_maps[0], incoming) + upper_maps[1]  24.4 us
    while x1, local copies, waits for them, and re-layouts, on_device(): lax.fori_loop(0, blocks - 1, lower_pass, jnp.zeros_like(lower_maps[1]))  15.6 us
  transfers between devices with their start and end apart: 36, of which 30 were waited for; matrix products, arithmetic and copies ran while one was open for 30% of the time, Pallas kernels for 0%

profile of v1, /device:TPU:24, one launch (start us, length us, event | category | flops | bytes accessed | tf_op | source)
XLA Modules:
  0.0 672.7 jit_solution(7881667384796818001)
XLA Ops:
  3.8 5.4 collective-permute-start.5
  13.0 4.2 all-to-all-start
  18.8 14.8 %copy.120 = f32[6,6,1,64,128]{1,0,4,3,2:T(8,128)} copy(f32[6,6,1,64,128]{4,3,2,1,0:T(8,128)} %get-tuple-element.420) | data formatting | bytes 2359296
  33.6 15.0 %copy.119 = f32[6,6,1,64,128]{0,1,4,3,2:T(8,128)} copy(f32[6,6,1,64,128]{4,3,2,1,0:T(8,128)} %get-tuple-element.419) | data formatting | bytes 2359296
  48.6 71.8 %fusion.17 = f32[6,6,64,128]{0,1,3,2:T(8,128)} fusion(f32[6,6,1,64,128]{0,1,4,3,2:T(8,128)} %copy.119, f32[6,6,1,64,128]{1,0,4,3,2:T(8,128)} %copy.120), kind=kOutput, calls=%fused_computation.28 | convolution fusion | flops 21233664 | bytes 3538944 | tf_op jit(solution)/shard_map/while/body/eval_jaxpr/ab...,bc...->ac.../dot_general | solution.py:44
  120.4 61.7 %fusion.12 = f32[6,6,64,128]{0,1,3,2:T(8,128)} fusion(f32[6,6,1,64,128]{1,0,4,3,2:T(8,128)} %copy.120, f32[6,6,1,64,128]{0,1,4,3,2:T(8,128)} %copy.119), kind=kOutput, calls=%fused_computation.27 | convolution fusion | flops 21233664 | bytes 3538944 | tf_op jit(solution)/shard_map/while/body/eval_jaxpr/ab...,bc...->ac.../dot_general | solution.py:44
  186.1 15.6 %copy.59 = f32[6,6,64,128]{3,2,1,0:T(8,128)} copy(f32[6,6,64,128]{0,1,3,2:T(8,128)} %fusion.17) | data formatting | bytes 2359296 | tf_op jit(solution)/shard_map/while | solution.py:85
  201.7 15.4 %copy.62 = f32[6,6,64,128]{3,2,1,0:T(8,128)} copy(f32[6,6,64,128]{0,1,3,2:T(8,128)} %fusion.12) | data formatting | bytes 2359296 | tf_op jit(solution)/shard_map/while | solution.py:111
  228.0 2.7 copy.121
  230.7 15.3 %fusion.4 = f32[64,128,6]{2,1,0:T(8,128)} fusion(f32[6,6,1,64,128]{1,0,4,3,2:T(8,128)} %copy.120, f32[64,128,6]{2,1,0:T(8,128)} %copy.121), kind=kLoop, calls=%fused_computation.19 | loop fusion | flops 540672 | bytes 1572864
  246.1 2.8 copy.100
  251.0 2.7 copy.122
  253.7 16.8 %fusion.3 = f32[64,128,6]{2,1,0:T(8,128)} fusion(f32[6,6,1,64,128]{0,1,4,3,2:T(8,128)} %copy.119, f32[64,128,6]{2,1,0:T(8,128)} %copy.122), kind=kLoop, calls=%fused_computation.16 | loop fusion | flops 540672 | bytes 1572864
  270.5 2.9 copy.107
  273.4 172.3 %while.65 = (s32[]{:T(128)}, f32[6,64,128]{2,1,0:T(8,128)S(1)}, f32[6,6,64,128]{3,2,1,0:T(8,128)}, f32[6,64,128]{2,1,0:T(8,128)S(1)}, s32[]{:T(128)}) while((s32[]{:T(128)}, f32[6,64,128]{2,1,0:T(8,128)S(1)}, f32[6,6,64,128]{3,2,1,0:T(8,128)}, f32[6,64,128]{2,1,0:T(8,128)S(1)}, s32[]{:T(128)}) %tuple.129), condition=%wide.region_1.3_spmd, body=%wide.region_0.2_spmd.sunk | while | flops 589826 | bytes 2949221 | solution.py:85
  274.9 3.5 collective-permute-start
  278.4 4.1 collective-permute-done
  283.9 5.6 collective-permute-start
  289.5 4.0 collective-permute-done
  294.9 6.5 collective-permute-start
  301.4 5.1 collective-permute-done
  308.0 6.5 collective-permute-start
  314.5 4.4 collective-permute-done
  320.3 6.5 collective-permute-start
  326.8 3.6 collective-permute-done
  331.8 6.5 collective-permute-start
  338.3 3.2 collective-permute-done
  343.0 6.5 collective-permute-start
  349.5 3.2 collective-permute-done
  354.1 6.5 collective-permute-start
  360.6 3.2 collective-permute-done
  365.2 6.5 collective-permute-start
  371.7 3.2 collective-permute-done
  376.3 6.5 collective-permute-start
  382.8 3.2 collective-permute-done
  387.4 6.5 collective-permute-start
  393.9 3.6 collective-permute-done
  399.0 6.5 collective-permute-start
  405.5 4.8 collective-permute-done
  411.7 6.5 collective-permute-start
  418.2 4.6 collective-permute-done
  424.3 6.5 collective-permute-start
  430.8 3.8 collective-permute-done
  436.0 6.5 collective-permute-start
  442.5 3.2 collective-permute-done
  449.7 15.4 %fusion.5 = f32[64,128,6]{2,1,0:T(8,128)} fusion(f32[6,6,1,64,128]{1,0,4,3,2:T(8,128)} %copy.120, f32[64,128,6]{2,1,0:T(8,128)} %copy.123), kind=kLoop, calls=%fused_computation.20 | loop fusion | flops 540672 | bytes 1572864
  465.2 3.6 copy.114
  471.2 195.3 %while.67 = (s32[]{:T(128)}, f32[6,64,128]{2,1,0:T(8,128)}, f32[6,6,64,128]{3,2,1,0:T(8,128)S(1)}, f32[6,64,128]{2,1,0:T(8,128)}, s32[]{:T(128)}) while((s32[]{:T(128)}, f32[6,64,128]{2,1,0:T(8,128)}, f32[6,6,64,128]{3,2,1,0:T(8,128)S(1)}, f32[6,64,128]{2,1,0:T(8,128)}, s32[]{:T(128)}) %tuple.128), condition=%wide.region_5.7_spmd, body=%wide.region_4.6_spmd.sunk | while | flops 589826 | bytes 2949221 | solution.py:111
  475.8 9.0 %collective-permute-done.1 = f32[6,64,128]{2,1,0:T(8,128)} collective-permute-done((f32[6,64,128]{2,1,0:T(8,128)}, f32[6,64,128]{2,1,0:T(8,128)}, u32[]{:S(2)}, u32[]{:S(2)}) %collective-permute-start.1) | collective-permute-done | bytes 196640 | tf_op jit(solution)/shard_map/while/body/eval_jaxpr/ppermute | solution.py:36
  489.4 8.1 %collective-permute-done.1 = f32[6,64,128]{2,1,0:T(8,128)} collective-permute-done((f32[6,64,128]{2,1,0:T(8,128)}, f32[6,64,128]{2,1,0:T(8,128)}, u32[]{:S(2)}, u32[]{:S(2)}) %collective-permute-start.1) | collective-permute-done | bytes 196640 | tf_op jit(solution)/shard_map/while/body/eval_jaxpr/ppermute | solution.py:36
  502.0 8.1 %collective-permute-done.1 = f32[6,64,128]{2,1,0:T(8,128)} collective-permute-done((f32[6,64,128]{2,1,0:T(8,128)}, f32[6,64,128]{2,1,0:T(8,128)}, u32[]{:S(2)}, u32[]{:S(2)}) %collective-permute-start.1) | collective-permute-done | bytes 196640 | tf_op jit(solution)/shard_map/while/body/eval_jaxpr/ppermute | solution.py:36
  514.7 8.1 %collective-permute-done.1 = f32[6,64,128]{2,1,0:T(8,128)} collective-permute-done((f32[6,64,128]{2,1,0:T(8,128)}, f32[6,64,128]{2,1,0:T(8,128)}, u32[]{:S(2)}, u32[]{:S(2)}) %collective-permute-start.1) | collective-permute-done | bytes 196640 | tf_op jit(solution)/shard_map/while/body/eval_jaxpr/ppermute | solution.py:36
  527.4 8.1 %collective-permute-done.1 = f32[6,64,128]{2,1,0:T(8,128)} collective-permute-done((f32[6,64,128]{2,1,0:T(8,128)}, f32[6,64,128]{2,1,0:T(8,128)}, u32[]{:S(2)}, u32[]{:S(2)}) %collective-permute-start.1) | collective-permute-done | bytes 196640 | tf_op jit(solution)/shard_map/while/body/eval_jaxpr/ppermute | solution.py:36
  540.1 8.1 %collective-permute-done.1 = f32[6,64,128]{2,1,0:T(8,128)} collective-permute-done((f32[6,64,128]{2,1,0:T(8,128)}, f32[6,64,128]{2,1,0:T(8,128)}, u32[]{:S(2)}, u32[]{:S(2)}) %collective-permute-start.1) | collective-permute-done | bytes 196640 | tf_op jit(solution)/shard_map/while/body/eval_jaxpr/ppermute | solution.py:36
  552.7 8.1 %collective-permute-done.1 = f32[6,64,128]{2,1,0:T(8,128)} collective-permute-done((f32[6,64,128]{2,1,0:T(8,128)}, f32[6,64,128]{2,1,0:T(8,128)}, u32[]{:S(2)}, u32[]{:S(2)}) %collective-permute-start.1) | collective-permute-done | bytes 196640 | tf_op jit(solution)/shard_map/while/body/eval_jaxpr/ppermute | solution.py:36
  565.4 8.1 %collective-permute-done.1 = f32[6,64,128]{2,1,0:T(8,128)} collective-permute-done((f32[6,64,128]{2,1,0:T(8,128)}, f32[6,64,128]{2,1,0:T(8,128)}, u32[]{:S(2)}, u32[]{:S(2)}) %collective-permute-start.1) | collective-permute-done | bytes 196640 | tf_op jit(solution)/shard_map/while/body/eval_jaxpr/ppermute | solution.py:36
  578.1 9.2 %collective-permute-done.1 = f32[6,64,128]{2,1,0:T(8,128)} collective-permute-done((f32[6,64,128]{2,1,0:T(8,128)}, f32[6,64,128]{2,1,0:T(8,128)}, u32[]{:S(2)}, u32[]{:S(2)}) %collective-permute-start.1) | collective-permute-done | bytes 196640 | tf_op jit(solution)/shard_map/while/body/eval_jaxpr/ppermute | solution.py:36
  591.9 10.0 %collective-permute-done.1 = f32[6,64,128]{2,1,0:T(8,128)} collective-permute-done((f32[6,64,128]{2,1,0:T(8,128)}, f32[6,64,128]{2,1,0:T(8,128)}, u32[]{:S(2)}, u32[]{:S(2)}) %collective-permute-start.1) | collective-permute-done | bytes 196640 | tf_op jit(solution)/shard_map/while/body/eval_jaxpr/ppermute | solution.py:36
  606.5 9.1 %collective-permute-done.1 = f32[6,64,128]{2,1,0:T(8,128)} collective-permute-done((f32[6,64,128]{2,1,0:T(8,128)}, f32[6,64,128]{2,1,0:T(8,128)}, u32[]{:S(2)}, u32[]{:S(2)}) %collective-permute-start.1) | collective-permute-done | bytes 196640 | tf_op jit(solution)/shard_map/while/body/eval_jaxpr/ppermute | solution.py:36
  620.2 8.3 %collective-permute-done.1 = f32[6,64,128]{2,1,0:T(8,128)} collective-permute-done((f32[6,64,128]{2,1,0:T(8,128)}, f32[6,64,128]{2,1,0:T(8,128)}, u32[]{:S(2)}, u32[]{:S(2)}) %collective-permute-start.1) | collective-permute-done | bytes 196640 | tf_op jit(solution)/shard_map/while/body/eval_jaxpr/ppermute | solution.py:36
  633.1 8.1 %collective-permute-done.1 = f32[6,64,128]{2,1,0:T(8,128)} collective-permute-done((f32[6,64,128]{2,1,0:T(8,128)}, f32[6,64,128]{2,1,0:T(8,128)}, u32[]{:S(2)}, u32[]{:S(2)}) %collective-permute-start.1) | collective-permute-done | bytes 196640 | tf_op jit(solution)/shard_map/while/body/eval_jaxpr/ppermute | solution.py:36
  645.8 8.1 %collective-permute-done.1 = f32[6,64,128]{2,1,0:T(8,128)} collective-permute-done((f32[6,64,128]{2,1,0:T(8,128)}, f32[6,64,128]{2,1,0:T(8,128)}, u32[]{:S(2)}, u32[]{:S(2)}) %collective-permute-start.1) | collective-permute-done | bytes 196640 | tf_op jit(solution)/shard_map/while/body/eval_jaxpr/ppermute | solution.py:36
  658.4 8.1 %collective-permute-done.1 = f32[6,64,128]{2,1,0:T(8,128)} collective-permute-done((f32[6,64,128]{2,1,0:T(8,128)}, f32[6,64,128]{2,1,0:T(8,128)}, u32[]{:S(2)}, u32[]{:S(2)}) %collective-permute-start.1) | collective-permute-done | bytes 196640 | tf_op jit(solution)/shard_map/while/body/eval_jaxpr/ppermute | solution.py:36
  666.5 5.4 while.68
  (141 shorter events, 129.5 us)
Async XLA Ops:
  0.0 17.2 %copy-start = (f32[6,6,2,64,128]{4,3,2,1,0:T(8,128)S(1)}, f32[6,6,2,64,128]{4,3,2,1,0:T(8,128)}, u32[]{:S(2)}) copy-start(f32[6,6,2,64,128]{4,3,2,1,0:T(8,128)} %param.21) | copy-start | bytes 7077892
  2.5 214.6 %collective-permute-start.4 = (f32[6,2,64,1]{3,0,2,1:T(8,128)}, f32[6,2,64,1]{3,0,2,1:T(8,128)S(1)}, u32[]{:S(2)}, u32[]{:S(2)}) collective-permute-start(f32[6,2,64,1]{3,0,2,1:T(8,128)} %get-tuple-element.423), channel_id=1, source_target_pairs={{1,0},{3,2},{5,4},{7,6},{9,8},{11,10},{13,12},{15,14},{17,16},{19,... | collective-permute-start | bytes 9224 | tf_op jit(solution)/shard_map/ppermute | solution.py:22
  3.8 213.4 %collective-permute-start.5 = (f32[6,2,64,1]{3,0,2,1:T(8,128)}, f32[6,2,64,1]{3,0,2,1:T(8,128)}, u32[]{:S(2)}, u32[]{:S(2)}) collective-permute-start(f32[6,2,64,1]{3,0,2,1:T(8,128)} %get-tuple-element.424), channel_id=1, source_target_pairs={{0,1},{2,3},{4,5},{6,7},{8,9},{10,11},{12,13},{14,15},{16,17},{18,... | collective-permute-start | bytes 9224 | tf_op jit(solution)/shard_map/ppermute | solution.py:21
  9.2 208.0 %collective-permute-start.2 = (f32[6,2,1,128]{3,0,2,1:T(8,128)S(1)}, f32[6,2,1,128]{3,0,2,1:T(8,128)S(1)}, u32[]{:S(2)}, u32[]{:S(2)}) collective-permute-start(f32[6,2,1,128]{3,0,2,1:T(8,128)S(1)} %get-tuple-element.421), channel_id=1, source_target_pairs={{2,0},{4,2},{6,4},{0,6},{3,1},{5,3},{7,5},{1,7},{10,8},{12,10},{14... | collective-permute-start | bytes 18440 | tf_op jit(solution)/shard_map/ppermute | solution.py:22
  13.0 169.1 %all-to-all-start = ((f32[4,6,64,128]{3,2,1,0:T(8,128)}), f32[4,6,64,128]{3,2,1,0:T(8,128)}, u32[]{:S(2)}, u32[]{:S(2)}) async-start(f32[4,6,64,128]{3,2,1,0:T(8,128)} %stack.3), calls=%async_computation | async-start | bytes 1572864 | tf_op jit(solution)/shard_map/all_to_all | solution.py:10
  120.4 61.7 %copy-start.8 = (s32[1,64]{1,0:T(1,128)S(1)}, s32[1,64]{1,0:T(1,128)}, u32[]{:S(2)}) copy-start(s32[1,64]{1,0:T(1,128)} %param.22) | copy-start | bytes 772
  120.4 65.5 %copy-start.7 = (f32[64]{0:T(128)S(1)}, f32[64]{0:T(128)}, u32[]{:S(2)}) copy-start(f32[64]{0:T(128)} %param.23) | copy-start | bytes 772
  184.3 35.5 %collective-permute-start.6 = (f32[6,256,128]{2,1,0:T(8,128)}, f32[6,256,128]{2,1,0:T(8,128)}, u32[]{:S(2)}, u32[]{:S(2)}) collective-permute-start(f32[6,256,128]{2,1,0:T(8,128)} %bitcast.33), channel_id=1, source_target_pairs={{120,0},{0,8},{8,16},{16,24},{24,32},{32,40},{40,48},{48,56},{56,6... | collective-permute-start | bytes 2359304 | tf_op jit(solution)/shard_map/ppermute | solution.py:30
  185.9 32.1 %collective-permute-start.3 = (f32[6,2,1,128]{3,0,2,1:T(8,128)S(1)}, f32[6,2,1,128]{3,0,2,1:T(8,128)S(1)}, u32[]{:S(2)}, u32[]{:S(2)}) collective-permute-start(f32[6,2,1,128]{3,0,2,1:T(8,128)S(1)} %get-tuple-element.422), channel_id=1, source_target_pairs={{0,2},{2,4},{4,6},{6,0},{1,3},{3,5},{5,7},{7,1},{8,10},{10,12},{12... | collective-permute-start | bytes 18440 | tf_op jit(solution)/shard_map/ppermute | solution.py:21
  201.7 16.2 %copy-start.6 = (f32[2,64,128]{2,1,0:T(8,128)S(1)}, f32[2,64,128]{2,1,0:T(8,128)}, u32[]{:S(2)}) copy-start(f32[2,64,128]{2,1,0:T(8,128)} %param.20) | copy-start | bytes 196612
  217.2 0.8 copy-start.4
  228.0 18.0 %copy-start.2 = (f32[6,2,64,128]{3,0,2,1:T(8,128)}, f32[6,2,64,128]{3,0,2,1:T(8,128)S(1)}, u32[]{:S(2)}) copy-start(f32[6,2,64,128]{3,0,2,1:T(8,128)S(1)} %get-tuple-element.415) | copy-start | bytes 1179652
  274.9 7.6 %collective-permute-start = (f32[6,64,128]{2,1,0:T(8,128)S(1)}, f32[6,64,128]{2,1,0:T(8,128)S(1)}, u32[]{:S(2)}, u32[]{:S(2)}) collective-permute-start(f32[6,64,128]{2,1,0:T(8,128)S(1)} %bitcast_add_fusion.8), channel_id=1, source_target_pairs={{0,8},{8,16},{16,24},{24,32},{32,40},{40,48},{48,56},{56,64},{64,7... | collective-permute-start | bytes 589832 | tf_op jit(solution)/shard_map/while/body/eval_jaxpr/ppermute | solution.py:36
  283.9 9.6 %collective-permute-start = (f32[6,64,128]{2,1,0:T(8,128)S(1)}, f32[6,64,128]{2,1,0:T(8,128)S(1)}, u32[]{:S(2)}, u32[]{:S(2)}) collective-permute-start(f32[6,64,128]{2,1,0:T(8,128)S(1)} %bitcast_add_fusion.8), channel_id=1, source_target_pairs={{0,8},{8,16},{16,24},{24,32},{32,40},{40,48},{48,56},{56,64},{64,7... | collective-permute-start | bytes 589832 | tf_op jit(solution)/shard_map/while/body/eval_jaxpr/ppermute | solution.py:36
  294.9 11.6 %collective-permute-start = (f32[6,64,128]{2,1,0:T(8,128)S(1)}, f32[6,64,128]{2,1,0:T(8,128)S(1)}, u32[]{:S(2)}, u32[]{:S(2)}) collective-permute-start(f32[6,64,128]{2,1,0:T(8,128)S(1)} %bitcast_add_fusion.8), channel_id=1, source_target_pairs={{0,8},{8,16},{16,24},{24,32},{32,40},{40,48},{48,56},{56,64},{64,7... | collective-permute-start | bytes 589832 | tf_op jit(solution)/shard_map/while/body/eval_jaxpr/ppermute | solution.py:36
  308.0 10.9 %collective-permute-start = (f32[6,64,128]{2,1,0:T(8,128)S(1)}, f32[6,64,128]{2,1,0:T(8,128)S(1)}, u32[]{:S(2)}, u32[]{:S(2)}) collective-permute-start(f32[6,64,128]{2,1,0:T(8,128)S(1)} %bitcast_add_fusion.8), channel_id=1, source_target_pairs={{0,8},{8,16},{16,24},{24,32},{32,40},{40,48},{48,56},{56,64},{64,7... | collective-permute-start | bytes 589832 | tf_op jit(solution)/shard_map/while/body/eval_jaxpr/ppermute | solution.py:36
  320.3 10.1 %collective-permute-start = (f32[6,64,128]{2,1,0:T(8,128)S(1)}, f32[6,64,128]{2,1,0:T(8,128)S(1)}, u32[]{:S(2)}, u32[]{:S(2)}) collective-permute-start(f32[6,64,128]{2,1,0:T(8,128)S(1)} %bitcast_add_fusion.8), channel_id=1, source_target_pairs={{0,8},{8,16},{16,24},{24,32},{32,40},{40,48},{48,56},{56,64},{64,7... | collective-permute-start | bytes 589832 | tf_op jit(solution)/shard_map/while/body/eval_jaxpr/ppermute | solution.py:36
  331.8 9.7 %collective-permute-start = (f32[6,64,128]{2,1,0:T(8,128)S(1)}, f32[6,64,128]{2,1,0:T(8,128)S(1)}, u32[]{:S(2)}, u32[]{:S(2)}) collective-permute-start(f32[6,64,128]{2,1,0:T(8,128)S(1)} %bitcast_add_fusion.8), channel_id=1, source_target_pairs={{0,8},{8,16},{16,24},{24,32},{32,40},{40,48},{48,56},{56,64},{64,7... | collective-permute-start | bytes 589832 | tf_op jit(solution)/shard_map/while/body/eval_jaxpr/ppermute | solution.py:36
  343.0 9.7 %collective-permute-start = (f32[6,64,128]{2,1,0:T(8,128)S(1)}, f32[6,64,128]{2,1,0:T(8,128)S(1)}, u32[]{:S(2)}, u32[]{:S(2)}) collective-permute-start(f32[6,64,128]{2,1,0:T(8,128)S(1)} %bitcast_add_fusion.8), channel_id=1, source_target_pairs={{0,8},{8,16},{16,24},{24,32},{32,40},{40,48},{48,56},{56,64},{64,7... | collective-permute-start | bytes 589832 | tf_op jit(solution)/shard_map/while/body/eval_jaxpr/ppermute | solution.py:36
  354.1 9.7 %collective-permute-start = (f32[6,64,128]{2,1,0:T(8,128)S(1)}, f32[6,64,128]{2,1,0:T(8,128)S(1)}, u32[]{:S(2)}, u32[]{:S(2)}) collective-permute-start(f32[6,64,128]{2,1,0:T(8,128)S(1)} %bitcast_add_fusion.8), channel_id=1, source_target_pairs={{0,8},{8,16},{16,24},{24,32},{32,40},{40,48},{48,56},{56,64},{64,7... | collective-permute-start | bytes 589832 | tf_op jit(solution)/shard_map/while/body/eval_jaxpr/ppermute | solution.py:36
  365.2 9.7 %collective-permute-start = (f32[6,64,128]{2,1,0:T(8,128)S(1)}, f32[6,64,128]{2,1,0:T(8,128)S(1)}, u32[]{:S(2)}, u32[]{:S(2)}) collective-permute-start(f32[6,64,128]{2,1,0:T(8,128)S(1)} %bitcast_add_fusion.8), channel_id=1, source_target_pairs={{0,8},{8,16},{16,24},{24,32},{32,40},{40,48},{48,56},{56,64},{64,7... | collective-permute-start | bytes 589832 | tf_op jit(solution)/shard_map/while/body/eval_jaxpr/ppermute | solution.py:36
  376.3 9.7 %collective-permute-start = (f32[6,64,128]{2,1,0:T(8,128)S(1)}, f32[6,64,128]{2,1,0:T(8,128)S(1)}, u32[]{:S(2)}, u32[]{:S(2)}) collective-permute-start(f32[6,64,128]{2,1,0:T(8,128)S(1)} %bitcast_add_fusion.8), channel_id=1, source_target_pairs={{0,8},{8,16},{16,24},{24,32},{32,40},{40,48},{48,56},{56,64},{64,7... | collective-permute-start | bytes 589832 | tf_op jit(solution)/shard_map/while/body/eval_jaxpr/ppermute | solution.py:36
  387.4 10.1 %collective-permute-start = (f32[6,64,128]{2,1,0:T(8,128)S(1)}, f32[6,64,128]{2,1,0:T(8,128)S(1)}, u32[]{:S(2)}, u32[]{:S(2)}) collective-permute-start(f32[6,64,128]{2,1,0:T(8,128)S(1)} %bitcast_add_fusion.8), channel_id=1, source_target_pairs={{0,8},{8,16},{16,24},{24,32},{32,40},{40,48},{48,56},{56,64},{64,7... | collective-permute-start | bytes 589832 | tf_op jit(solution)/shard_map/while/body/eval_jaxpr/ppermute | solution.py:36
  399.0 11.3 %collective-permute-start = (f32[6,64,128]{2,1,0:T(8,128)S(1)}, f32[6,64,128]{2,1,0:T(8,128)S(1)}, u32[]{:S(2)}, u32[]{:S(2)}) collective-permute-start(f32[6,64,128]{2,1,0:T(8,128)S(1)} %bitcast_add_fusion.8), channel_id=1, source_target_pairs={{0,8},{8,16},{16,24},{24,32},{32,40},{40,48},{48,56},{56,64},{64,7... | collective-permute-start | bytes 589832 | tf_op jit(solution)/shard_map/while/body/eval_jaxpr/ppermute | solution.py:36
  411.7 11.1 %collective-permute-start = (f32[6,64,128]{2,1,0:T(8,128)S(1)}, f32[6,64,128]{2,1,0:T(8,128)S(1)}, u32[]{:S(2)}, u32[]{:S(2)}) collective-permute-start(f32[6,64,128]{2,1,0:T(8,128)S(1)} %bitcast_add_fusion.8), channel_id=1, source_target_pairs={{0,8},{8,16},{16,24},{24,32},{32,40},{40,48},{48,56},{56,64},{64,7... | collective-permute-start | bytes 589832 | tf_op jit(solution)/shard_map/while/body/eval_jaxpr/ppermute | solution.py:36
  424.3 10.3 %collective-permute-start = (f32[6,64,128]{2,1,0:T(8,128)S(1)}, f32[6,64,128]{2,1,0:T(8,128)S(1)}, u32[]{:S(2)}, u32[]{:S(2)}) collective-permute-start(f32[6,64,128]{2,1,0:T(8,128)S(1)} %bitcast_add_fusion.8), channel_id=1, source_target_pairs={{0,8},{8,16},{16,24},{24,32},{32,40},{40,48},{48,56},{56,64},{64,7... | collective-permute-start | bytes 589832 | tf_op jit(solution)/shard_map/while/body/eval_jaxpr/ppermute | solution.py:36
  436.0 9.7 %collective-permute-start = (f32[6,64,128]{2,1,0:T(8,128)S(1)}, f32[6,64,128]{2,1,0:T(8,128)S(1)}, u32[]{:S(2)}, u32[]{:S(2)}) collective-permute-start(f32[6,64,128]{2,1,0:T(8,128)S(1)} %bitcast_add_fusion.8), channel_id=1, source_target_pairs={{0,8},{8,16},{16,24},{24,32},{32,40},{40,48},{48,56},{56,64},{64,7... | collective-permute-start | bytes 589832 | tf_op jit(solution)/shard_map/while/body/eval_jaxpr/ppermute | solution.py:36
  446.1 3.6 copy-start.3
  465.1 6.0 copy-start.1
  473.9 10.9 %collective-permute-start.1 = (f32[6,64,128]{2,1,0:T(8,128)}, f32[6,64,128]{2,1,0:T(8,128)}, u32[]{:S(2)}, u32[]{:S(2)}) collective-permute-start(f32[6,64,128]{2,1,0:T(8,128)} %bitcast_add_fusion.9), channel_id=1, source_target_pairs={{8,0},{16,8},{24,16},{32,24},{40,32},{48,40},{56,48},{64,56},{72,6... | collective-permute-start | bytes 589832 | tf_op jit(solution)/shard_map/while/body/eval_jaxpr/ppermute | solution.py:36
  487.4 10.0 %collective-permute-start.1 = (f32[6,64,128]{2,1,0:T(8,128)}, f32[6,64,128]{2,1,0:T(8,128)}, u32[]{:S(2)}, u32[]{:S(2)}) collective-permute-start(f32[6,64,128]{2,1,0:T(8,128)} %bitcast_add_fusion.9), channel_id=1, source_target_pairs={{8,0},{16,8},{24,16},{32,24},{40,32},{48,40},{56,48},{64,56},{72,6... | collective-permute-start | bytes 589832 | tf_op jit(solution)/shard_map/while/body/eval_jaxpr/ppermute | solution.py:36
  500.1 10.0 %collective-permute-start.1 = (f32[6,64,128]{2,1,0:T(8,128)}, f32[6,64,128]{2,1,0:T(8,128)}, u32[]{:S(2)}, u32[]{:S(2)}) collective-permute-start(f32[6,64,128]{2,1,0:T(8,128)} %bitcast_add_fusion.9), channel_id=1, source_target_pairs={{8,0},{16,8},{24,16},{32,24},{40,32},{48,40},{56,48},{64,56},{72,6... | collective-permute-start | bytes 589832 | tf_op jit(solution)/shard_map/while/body/eval_jaxpr/ppermute | solution.py:36
  512.8 10.0 %collective-permute-start.1 = (f32[6,64,128]{2,1,0:T(8,128)}, f32[6,64,128]{2,1,0:T(8,128)}, u32[]{:S(2)}, u32[]{:S(2)}) collective-permute-start(f32[6,64,128]{2,1,0:T(8,128)} %bitcast_add_fusion.9), channel_id=1, source_target_pairs={{8,0},{16,8},{24,16},{32,24},{40,32},{48,40},{56,48},{64,56},{72,6... | collective-permute-start | bytes 589832 | tf_op jit(solution)/shard_map/while/body/eval_jaxpr/ppermute | solution.py:36
  525.5 10.0 %collective-permute-start.1 = (f32[6,64,128]{2,1,0:T(8,128)}, f32[6,64,128]{2,1,0:T(8,128)}, u32[]{:S(2)}, u32[]{:S(2)}) collective-permute-start(f32[6,64,128]{2,1,0:T(8,128)} %bitcast_add_fusion.9), channel_id=1, source_target_pairs={{8,0},{16,8},{24,16},{32,24},{40,32},{48,40},{56,48},{64,56},{72,6... | collective-permute-start | bytes 589832 | tf_op jit(solution)/shard_map/while/body/eval_jaxpr/ppermute | solution.py:36
  538.1 10.0 %collective-permute-start.1 = (f32[6,64,128]{2,1,0:T(8,128)}, f32[6,64,128]{2,1,0:T(8,128)}, u32[]{:S(2)}, u32[]{:S(2)}) collective-permute-start(f32[6,64,128]{2,1,0:T(8,128)} %bitcast_add_fusion.9), channel_id=1, source_target_pairs={{8,0},{16,8},{24,16},{32,24},{40,32},{48,40},{56,48},{64,56},{72,6... | collective-permute-start | bytes 589832 | tf_op jit(solution)/shard_map/while/body/eval_jaxpr/ppermute | solution.py:36
  550.8 10.0 %collective-permute-start.1 = (f32[6,64,128]{2,1,0:T(8,128)}, f32[6,64,128]{2,1,0:T(8,128)}, u32[]{:S(2)}, u32[]{:S(2)}) collective-permute-start(f32[6,64,128]{2,1,0:T(8,128)} %bitcast_add_fusion.9), channel_id=1, source_target_pairs={{8,0},{16,8},{24,16},{32,24},{40,32},{48,40},{56,48},{64,56},{72,6... | collective-permute-start | bytes 589832 | tf_op jit(solution)/shard_map/while/body/eval_jaxpr/ppermute | solution.py:36
  563.5 10.0 %collective-permute-start.1 = (f32[6,64,128]{2,1,0:T(8,128)}, f32[6,64,128]{2,1,0:T(8,128)}, u32[]{:S(2)}, u32[]{:S(2)}) collective-permute-start(f32[6,64,128]{2,1,0:T(8,128)} %bitcast_add_fusion.9), channel_id=1, source_target_pairs={{8,0},{16,8},{24,16},{32,24},{40,32},{48,40},{56,48},{64,56},{72,6... | collective-permute-start | bytes 589832 | tf_op jit(solution)/shard_map/while/body/eval_jaxpr/ppermute | solution.py:36
  576.2 11.1 %collective-permute-start.1 = (f32[6,64,128]{2,1,0:T(8,128)}, f32[6,64,128]{2,1,0:T(8,128)}, u32[]{:S(2)}, u32[]{:S(2)}) collective-permute-start(f32[6,64,128]{2,1,0:T(8,128)} %bitcast_add_fusion.9), channel_id=1, source_target_pairs={{8,0},{16,8},{24,16},{32,24},{40,32},{48,40},{56,48},{64,56},{72,6... | collective-permute-start | bytes 589832 | tf_op jit(solution)/shard_map/while/body/eval_jaxpr/ppermute | solution.py:36
  590.0 11.9 %collective-permute-start.1 = (f32[6,64,128]{2,1,0:T(8,128)}, f32[6,64,128]{2,1,0:T(8,128)}, u32[]{:S(2)}, u32[]{:S(2)}) collective-permute-start(f32[6,64,128]{2,1,0:T(8,128)} %bitcast_add_fusion.9), channel_id=1, source_target_pairs={{8,0},{16,8},{24,16},{32,24},{40,32},{48,40},{56,48},{64,56},{72,6... | collective-permute-start | bytes 589832 | tf_op jit(solution)/shard_map/while/body/eval_jaxpr/ppermute | solution.py:36
  604.6 11.0 %collective-permute-start.1 = (f32[6,64,128]{2,1,0:T(8,128)}, f32[6,64,128]{2,1,0:T(8,128)}, u32[]{:S(2)}, u32[]{:S(2)}) collective-permute-start(f32[6,64,128]{2,1,0:T(8,128)} %bitcast_add_fusion.9), channel_id=1, source_target_pairs={{8,0},{16,8},{24,16},{32,24},{40,32},{48,40},{56,48},{64,56},{72,6... | collective-permute-start | bytes 589832 | tf_op jit(solution)/shard_map/while/body/eval_jaxpr/ppermute | solution.py:36
  618.3 10.2 %collective-permute-start.1 = (f32[6,64,128]{2,1,0:T(8,128)}, f32[6,64,128]{2,1,0:T(8,128)}, u32[]{:S(2)}, u32[]{:S(2)}) collective-permute-start(f32[6,64,128]{2,1,0:T(8,128)} %bitcast_add_fusion.9), channel_id=1, source_target_pairs={{8,0},{16,8},{24,16},{32,24},{40,32},{48,40},{56,48},{64,56},{72,6... | collective-permute-start | bytes 589832 | tf_op jit(solution)/shard_map/while/body/eval_jaxpr/ppermute | solution.py:36
  631.2 10.0 %collective-permute-start.1 = (f32[6,64,128]{2,1,0:T(8,128)}, f32[6,64,128]{2,1,0:T(8,128)}, u32[]{:S(2)}, u32[]{:S(2)}) collective-permute-start(f32[6,64,128]{2,1,0:T(8,128)} %bitcast_add_fusion.9), channel_id=1, source_target_pairs={{8,0},{16,8},{24,16},{32,24},{40,32},{48,40},{56,48},{64,56},{72,6... | collective-permute-start | bytes 589832 | tf_op jit(solution)/shard_map/while/body/eval_jaxpr/ppermute | solution.py:36
  643.8 10.0 %collective-permute-start.1 = (f32[6,64,128]{2,1,0:T(8,128)}, f32[6,64,128]{2,1,0:T(8,128)}, u32[]{:S(2)}, u32[]{:S(2)}) collective-permute-start(f32[6,64,128]{2,1,0:T(8,128)} %bitcast_add_fusion.9), channel_id=1, source_target_pairs={{8,0},{16,8},{24,16},{32,24},{40,32},{48,40},{56,48},{64,56},{72,6... | collective-permute-start | bytes 589832 | tf_op jit(solution)/shard_map/while/body/eval_jaxpr/ppermute | solution.py:36
  656.5 10.0 %collective-permute-start.1 = (f32[6,64,128]{2,1,0:T(8,128)}, f32[6,64,128]{2,1,0:T(8,128)}, u32[]{:S(2)}, u32[]{:S(2)}) collective-permute-start(f32[6,64,128]{2,1,0:T(8,128)} %bitcast_add_fusion.9), channel_id=1, source_target_pairs={{8,0},{16,8},{24,16},{32,24},{40,32},{48,40},{56,48},{64,56},{72,6... | collective-permute-start | bytes 589832 | tf_op jit(solution)/shard_map/while/body/eval_jaxpr/ppermute | solution.py:36
  672.0 0.7 copy-start.5
